TPU v7x, 256 devices: a whole 4x4x8 slice. The times are simulated.
256 devices in a mesh: region: 16 (over z_lo, x, core), member: 16 (over y, z_hi).
Axes of the slice: x: 4, y: 4, z: 8 (z_hi: 4, z_lo: 2; z = z_hi * 2 + z_lo), core: 2. Of those that a mesh axis runs over, the one named last changes fastest.
Arguments:
- predicted_states: float32 [32, 100, 512, 128], P('member', None, 'region'), may hold values from -20 to 20, as said below
- observed_analysis: float32 [100, 512, 128], P(None, 'region'), may hold values from -20 to 20
- tile_location_sequence: int32 [16, 4096], P('region'), may hold values from 0 to 4095, each once within a row
Outputs:
- gradient: float32 [32, 100, 512, 128], P('member', None, 'region')
Inputs may be any that keep to these rules, and one draw needn't show every extreme that they name: Each row of tile_location_sequence is a permutation of the cells of one region. `predicted_states`: members share a common field per variable and cell, with variable and cell scales.
All inputs are finite; a program needn't handle non-finite values.
Results may differ from a plain program's by a relative error of at most 0.0003.
Values sent between devices are 32-bit elements; how exact they have to be, the bound alone decides.
A program may use at most 128 MiB of HBM per device.

v0:
```python
import jax
import jax.numpy as jnp
from jax import lax
from jax.sharding import PartitionSpec as P

LON = 128
HALF = 32
PATCH = 128


def extended(block, sides, width):
    for axis, dim in sides:
        count = lax.axis_size(axis)
        forward = [(i, i + 1) for i in range(count - 1)]
        backward = [(target, source) for source, target in forward]
        low = lax.ppermute(
            lax.slice_in_dim(block, block.shape[dim] - width, None, axis=dim), axis, forward
        )
        high = lax.ppermute(lax.slice_in_dim(block, 0, width, axis=dim), axis, backward)
        block = jnp.concatenate([low, block, high], axis=dim)
    return block


def kernel_value(offset, half):
    sigma = half / 2.0
    steps = jnp.arange(-half, half + 1).astype(jnp.float32)
    norm_sum = jnp.sum(jnp.exp(-(steps * steps) / (2.0 * sigma * sigma)))
    bell = jnp.exp(-(offset * offset) / (2.0 * sigma * sigma)) / norm_sum
    value = 0.5 * (offset == 0.0).astype(jnp.float32) + 0.5 * bell
    return jnp.where(jnp.abs(offset) <= half, value, jnp.zeros_like(value))


def lon_matrix():
    first = jnp.arange(LON)[:, None]
    second = jnp.arange(LON)[None, :]
    offset = second - first
    return kernel_value(offset.astype(jnp.float32), HALF)


def band_rows(along_lon):
    padded = extended(along_lon, (("region", 2),), HALF)
    local_rows = along_lon.shape[2]
    out_rows = jnp.arange(local_rows)[:, None]
    in_rows = jnp.arange(local_rows + 2 * HALF)[None, :]
    lat_band = kernel_value((in_rows - HALF - out_rows).astype(jnp.float32), HALF)
    return jnp.einsum("rp,mvpk->mvrk", lat_band, padded, precision=lax.Precision.HIGHEST)


def smooth_surface(values):
    along_lon = jnp.einsum("mvrl,lk->mvrk", values, lon_matrix(), precision=lax.Precision.HIGHEST)
    return band_rows(along_lon)


def pair_terms(gathered):
    members = gathered.shape[0]
    inner_products = jnp.einsum(
        "mvkp,nvkp->vkmn", gathered, gathered, precision=lax.Precision.HIGHEST
    )
    squares = jnp.einsum("mvkp,mvkp->vkm", gathered, gathered, precision=lax.Precision.HIGHEST)
    dist_sq = jnp.maximum(
        squares[:, :, :, None] + squares[:, :, None, :] - 2.0 * inner_products, 0.0
    )
    self_pair = jnp.arange(members)[:, None] == jnp.arange(members)[None, :]
    pair_weights = jnp.where(
        self_pair[None, None], jnp.zeros_like(dist_sq), 1.0 / jnp.sqrt(dist_sq + 1e-06)
    )
    pulled = jnp.transpose(jnp.sum(pair_weights, axis=-1), (2, 0, 1))
    apart = pulled[..., None] * gathered - jnp.einsum(
        "vkmn,nvkp->mvkp", pair_weights, gathered, precision=lax.Precision.HIGHEST
    )
    apart = apart / members
    return lax.all_to_all(apart, "member", split_axis=0, concat_axis=2, tiled=True)


def reorder_cells(values, positions):
    cell_count = values.shape[-1]
    flattened = values.reshape(-1, cell_count).T
    reordered = jnp.take(flattened, positions, axis=0)
    return reordered.T.reshape(values.shape)


def on_device(predicted_states, observed_analysis, tile_location_sequence):
    local_ensemble_copies = predicted_states.shape[0]
    quantity_names = predicted_states.shape[1]
    mesh_locations = predicted_states.shape[2] * predicted_states.shape[3]
    blocks = mesh_locations // PATCH
    order = tile_location_sequence[0]
    inverse_order = (
        jnp.zeros((mesh_locations,), jnp.int32).at[order].set(jnp.arange(mesh_locations))
    )
    softened_surface = smooth_surface(predicted_states)
    picked = reorder_cells(
        softened_surface.reshape(local_ensemble_copies, quantity_names, mesh_locations), order
    )
    picked = picked.reshape(local_ensemble_copies, quantity_names, blocks, PATCH)
    truth = reorder_cells(observed_analysis.reshape(quantity_names, mesh_locations), order).reshape(
        quantity_names, blocks, PATCH
    )
    diff = picked - truth[None]
    toward = diff / jnp.sqrt(jnp.sum(diff * diff, axis=-1, keepdims=True) + 1e-06)
    apart = pair_terms(lax.all_to_all(picked, "member", split_axis=2, concat_axis=0, tiled=True))
    patch_grad = jnp.sqrt(jnp.float32(PATCH)) * (toward - apart)
    located_points = reorder_cells(
        patch_grad.reshape(local_ensemble_copies, quantity_names, mesh_locations), inverse_order
    )
    return smooth_surface(located_points.reshape(predicted_states.shape))


def solution(mesh):
    in_specs = (P("member", None, "region", None), P(None, "region", None), P("region", None))
    out_specs = P("member", None, "region", None)
    return jax.shard_map(
        on_device, mesh=mesh, in_specs=in_specs, out_specs=out_specs, check_vma=False
    )
```

profile of v0, /device:TPU:1, one launch (start us, length us, event | category | flops | bytes accessed | tf_op | source)
XLA Modules:
  0.0 415.7 jit_solution(14891175216338866984)
XLA Ops:
  1.9 5.8 %fusion.14 = f32[2,100,32,128]{3,1,2,0:T(8,128)S(1)} fusion(f32[2,100,32,128]{3,2,1,0:T(8,128)S(1)} %copy-done, f32[]{:T(128)} %exponential_reduce_fusion), kind=kOutput, calls=%fused_computation.29 | convolution fusion | flops 1258504192 | bytes 6553604 | tf_op jit(solution)/shard_map/mvrl,lk->mvrk/dot_general | solution.py:50
  9.4 4.5 %collective-permute-start = (f32[2,100,32,128]{3,2,1,0:T(8,128)S(1)}, f32[2,100,32,128]{3,2,1,0:T(8,128)S(1)}, u32[]{:S(2)}, u32[]{:S(2)}) collective-permute-start(f32[2,100,32,128]{3,2,1,0:T(8,128)S(1)} %copy.65), channel_id=1, source_target_pairs={{0,16},{16,32},{32,48},{48,64},{64,80},{80,96},{96,112},{112,128},... | collective-permute-start | bytes 9830408 | tf_op jit(solution)/shard_map/ppermute | solution.py:16
  16.3 33.2 %collective-permute-done = f32[2,100,32,128]{3,2,1,0:T(8,128)S(1)} collective-permute-done((f32[2,100,32,128]{3,2,1,0:T(8,128)S(1)}, f32[2,100,32,128]{3,2,1,0:T(8,128)S(1)}, u32[]{:S(2)}, u32[]{:S(2)}) %collective-permute-start) | collective-permute-done | bytes 3276832 | tf_op jit(solution)/shard_map/ppermute | solution.py:16
  49.5 3.6 copy.67
  53.9 3.7 copy.68
  57.7 8.5 %pad_maximum_fusion = f32[2,100,96,128]{3,1,2,0:T(8,128)} fusion(f32[2,100,32,128]{3,1,2,0:T(8,128)} %copy.68, f32[2,100,32,128]{3,1,2,0:T(8,128)} %copy-done.2, f32[2,100,32,128]{3,1,2,0:T(8,128)} %copy.67), kind=kLoop, calls=%fused_computation.4 | loop fusion | flops 4915200 | bytes 19660800 | tf_op jit(solution)/shard_map/concatenate | solution.py:20
  66.2 10.9 %fusion.6 = f32[2,100,128,32]{2,3,1,0:T(8,128)S(1)} fusion(f32[2,100,96,128]{3,1,2,0:T(8,128)} %pad_maximum_fusion, f32[]{:T(128)} %exponential_reduce_fusion, s32[96]{0:T(128)S(1)} %iota_add_fusion), kind=kOutput, calls=%fused_computation.11 | convolution fusion | flops 943758336 | bytes 13107588 | tf_op jit(solution)/shard_map/rp,mvpk->mvrk/dot_general | solution.py:46
  80.0 3.3 copy.70
  83.3 18.3 %gather_fusion.1 = f32[4096,200]{1,0:T(8,128)} fusion(f32[4096,200]{1,0:T(8,128)} %bitcast.86, s32[4096]{0:T(1024)S(1)} %fusion.25), kind=kCustom, calls=%fused_computation.clone | custom fusion | bytes 6569984 | tf_op jit(solution)/shard_map/jit(_take)/gather | solution.py:78
  101.6 3.7 copy.71
  107.9 4.2 %copy.74 = f32[2,100,32,128]{3,0,1,2:T(2,128)} copy(f32[2,100,32,128]{3,2,1,0:T(8,128)S(1)} %bitcast.91) | data formatting | bytes 6553600 | tf_op jit(solution)/shard_map/reshape;reshape | solution.py:95
  112.1 11.4 %all-to-all-start = ((f32[2,100,32,128]{3,0,1,2:T(2,128)}), f32[2,100,32,128]{3,0,1,2:T(2,128)S(1)}, u32[]{:S(2)}, u32[]{:S(2)}) async-start(f32[2,100,32,128]{3,0,1,2:T(2,128)} %copy.74), calls=%async_computation | async-start | bytes 6553600 | tf_op jit(solution)/shard_map/all_to_all | solution.py:101
  123.5 54.1 %all-to-all-done = f32[2,100,32,128]{3,0,1,2:T(2,128)S(1)} async-done(((f32[2,100,32,128]{3,0,1,2:T(2,128)}), f32[2,100,32,128]{3,0,1,2:T(2,128)S(1)}, u32[]{:S(2)}, u32[]{:S(2)}) %all-to-all-start) | async-done | bytes 3276832 | tf_op jit(solution)/shard_map/all_to_all | solution.py:101
  182.5 6.2 %fusion.46 = (f32[100,2,32]{2,1,0:T(2,128)S(1)}, f32[100,2,32,32]{2,3,1,0:T(8,128)S(1)}) fusion(f32[32,100,2,128]{3,0,2,1:T(8,128)S(1)} %bitcast.89, f32[100,2,32]{2,1,0:T(2,128)S(1)} %multiply_reduce_fusion, pred[32,32]{0,1:T(8,128)(4,1)S(1)} %iota_compare_fusion), kind=kOutput, calls=%fused_computation.74 | convolution fusion | flops 316000000 | bytes 4148224 | tf_op jit(solution)/shard_map/mvkp,nvkp->vkmn/dot_general | solution.py:56
  188.7 6.6 %fusion.13 = f32[32,100,2,128]{3,0,2,1:T(8,128)S(1)} fusion(f32[32,100,2,128]{3,0,2,1:T(8,128)S(1)} %bitcast.90, f32[100,2,32,32]{2,3,1,0:T(8,128)S(1)} %get-tuple-element.7, f32[32,100,2]{0,2,1:T(2,128)S(1)} %bitcast.102), kind=kOutput, calls=%fused_computation.23 | convolution fusion | flops 317030400 | bytes 7398400 | tf_op jit(solution)/shard_map/vkmn,nvkp->mvkp/dot_general | solution.py:68
  195.3 4.2 %copy.78 = f32[32,100,2,128]{3,2,1,0:T(2,128)} copy(f32[32,100,2,128]{3,0,2,1:T(8,128)S(1)} %fusion.13) | data formatting | bytes 6553600 | tf_op jit(solution)/shard_map/div | solution.py:71
  199.6 4.5 %all-to-all-start.1 = ((f32[32,100,2,128]{3,2,1,0:T(2,128)}), f32[32,100,2,128]{3,2,1,0:T(2,128)}, u32[]{:S(2)}, u32[]{:S(2)}) async-start(f32[32,100,2,128]{3,2,1,0:T(2,128)} %copy.78), calls=%async_computation.1 | async-start | bytes 6553600 | tf_op jit(solution)/shard_map/all_to_all | solution.py:72
  206.0 14.1 %gather_fusion = f32[4096,100]{1,0:T(8,128)} fusion(f32[4096,100]{1,0:T(8,128)S(1)} %bitcast.87, s32[4096]{0:T(1024)S(1)} %broadcast_clamp_fusion), kind=kCustom, calls=%fused_computation.2 | custom fusion | bytes 3293184 | tf_op jit(solution)/shard_map/jit(_take)/gather | solution.py:78
  220.1 4.8 %broadcast_select_fusion = f32[4096,100]{1,0:T(8,128)} fusion(f32[4096,100]{1,0:T(8,128)} %gather_fusion, pred[4096]{0:T(1024)(128)(4,1)S(1)} %compare_and_fusion.1), kind=kLoop, calls=%fused_computation.31 | loop fusion | flops 409600 | bytes 3280896 | tf_op jit(solution)/shard_map/jit(_take)/select_n | solution.py:78
  228.0 15.7 %scatter_custom_fusion = s32[4096]{0:T(1024)S(1)} fusion(s32[4096]{0:T(1024)S(1)} %bitcast.106, s32[4096]{0:T(1024)S(1)} %iota.49, s32[]{:T(128)} %constant.26.clone.1), kind=kCustom, calls=%fused_computation.53 | custom fusion | bytes 16388 | tf_op jit(solution)/shard_map/scatter | solution.py:89
  246.2 3.8 copy.106
  250.0 4.3 %all_to_all.33 = f32[200,4096]{1,0:T(8,128)} reshape(f32[2,100,16,2,128]{4,3,2,1,0:T(2,128)S(1)} %bitcast.97) | data formatting | bytes 6553600 | tf_op jit(solution)/shard_map/all_to_all | solution.py:72
  258.0 8.6 %fusion.12 = f32[4096,200]{0,1:T(8,128)} fusion(f32[200,4096]{1,0:T(8,128)S(1)} %copy-done.8, f32[25,8,32,128]{3,2,1,0:T(8,128)S(1)} %bitcast.98, f32[25,8,32,128]{3,2,1,0:T(8,128)S(1)} %bitcast.99, f32[4096,200]{0,1:T(8,128)S(1)} %copy-done.6, pred[4096]{0:T(1024)(128)(4,1)S(1)} %compare_and_fusion.1), kind=kLoop, calls=%fused_computation.19 | loop fusion | flops 4096000 | bytes 16388096 | tf_op jit(solution)/shard_map/transpose | solution.py:77
  266.6 5.2 %copy.80 = f32[4096,200]{1,0:T(8,128)} copy(f32[4096,200]{0,1:T(8,128)} %fusion.12) | data formatting | bytes 6553600 | tf_op jit(solution)/shard_map/transpose | solution.py:77
  271.8 18.3 %gather_fusion.2 = f32[4096,200]{1,0:T(8,128)} fusion(f32[4096,200]{1,0:T(8,128)} %copy.80, s32[4096]{0:T(1024)S(1)} %fusion.26), kind=kCustom, calls=%fused_computation.1.clone | custom fusion | bytes 6569984 | tf_op jit(solution)/shard_map/jit(_take)/gather | solution.py:78
  290.1 3.9 select_bitcast_fusion
  294.0 5.3 %copy.81 = f32[200,4096]{1,0:T(8,128)} copy(f32[200,4096]{0,1:T(8,128)} %select_bitcast_fusion) | data formatting | bytes 6553600 | tf_op jit(solution)/shard_map/transpose | solution.py:79
  301.8 3.4 fusion.20
  305.2 61.9 %collective-permute-start.2 = (f32[2,100,32,128]{3,2,1,0:T(8,128)S(1)}, f32[2,100,32,128]{3,2,1,0:T(8,128)S(1)}, u32[]{:S(2)}, u32[]{:S(2)}) collective-permute-start(f32[2,100,32,128]{3,2,1,0:T(8,128)S(1)} %fusion.20), channel_id=1, source_target_pairs={{0,16},{16,32},{32,48},{48,64},{64,80},{80,96},{96,112},{112,128},... | collective-permute-start | bytes 9830408 | tf_op jit(solution)/shard_map/ppermute | solution.py:16
  369.1 33.7 %collective-permute-done.2 = f32[2,100,32,128]{3,2,1,0:T(8,128)S(1)} collective-permute-done((f32[2,100,32,128]{3,2,1,0:T(8,128)S(1)}, f32[2,100,32,128]{3,2,1,0:T(8,128)S(1)}, u32[]{:S(2)}, u32[]{:S(2)}) %collective-permute-start.2) | collective-permute-done | bytes 3276832 | tf_op jit(solution)/shard_map/ppermute | solution.py:16
  402.8 4.4 %collective-permute-done.3 = f32[2,100,32,128]{3,2,1,0:T(8,128)S(1)} collective-permute-done((f32[2,100,32,128]{3,2,1,0:T(8,128)S(1)}, f32[2,100,32,128]{3,2,1,0:T(8,128)S(1)}, u32[]{:S(2)}, u32[]{:S(2)}) %collective-permute-start.3) | collective-permute-done | bytes 3276832 | tf_op jit(solution)/shard_map/ppermute | solution.py:19
  407.2 8.0 %fusion.17 = f32[2,100,32,128]{3,2,1,0:T(8,128)} fusion(f32[2,100,32,128]{3,2,1,0:T(8,128)S(1)} %collective-permute-done.3, f32[2,100,32,128]{3,2,1,0:T(8,128)S(1)} %fusion.20, f32[2,100,32,128]{3,2,1,0:T(8,128)S(1)} %collective-permute-done.2, f32[]{:T(128)} %exponential_reduce_fusion, s32[96]{0:T(128)S(1)} %iota_add_fusion), kind=kOutput, calls=%fused_computation.30 | convolution fusion | flops 948673536 | bytes 13107588 | tf_op jit(solution)/shard_map/rp,mvpk->mvrk/dot_general | solution.py:46
  (48 shorter events, 32.3 us)
Async XLA Ops:
  0.0 1.9 copy-start
  7.7 1.7 copy-start.2
  7.7 8.5 %copy-start.9 = (s32[1,4096]{1,0:T(1,128)S(1)}, s32[1,4096]{1,0:T(1,128)}, u32[]{:S(2)}) copy-start(s32[1,4096]{1,0:T(1,128)} %param.7) | copy-start | bytes 49156
  9.4 40.1 %collective-permute-start = (f32[2,100,32,128]{3,2,1,0:T(8,128)S(1)}, f32[2,100,32,128]{3,2,1,0:T(8,128)S(1)}, u32[]{:S(2)}, u32[]{:S(2)}) collective-permute-start(f32[2,100,32,128]{3,2,1,0:T(8,128)S(1)} %copy.65), channel_id=1, source_target_pairs={{0,16},{16,32},{32,48},{48,64},{64,80},{80,96},{96,112},{112,128},... | collective-permute-start | bytes 9830408 | tf_op jit(solution)/shard_map/ppermute | solution.py:16
  13.9 40.0 %collective-permute-start.1 = (f32[2,100,32,128]{3,2,1,0:T(8,128)S(1)}, f32[2,100,32,128]{3,2,1,0:T(8,128)S(1)}, u32[]{:S(2)}, u32[]{:S(2)}) collective-permute-start(f32[2,100,32,128]{3,2,1,0:T(8,128)S(1)} %copy.65), channel_id=1, source_target_pairs={{16,0},{32,16},{48,32},{64,48},{80,64},{96,80},{112,96},{128,112},... | collective-permute-start | bytes 9830408 | tf_op jit(solution)/shard_map/ppermute | solution.py:19
  105.3 1.7 copy-start.5
  107.9 4.2 %copy-start.3 = (f32[25,8,32,128]{3,2,1,0:T(8,128)}, f32[25,8,32,128]{3,2,1,0:T(8,128)S(1)}, u32[]{:S(2)}) copy-start(f32[25,8,32,128]{3,2,1,0:T(8,128)S(1)} %copy.92) | copy-start | bytes 9830404
  112.1 65.5 %all-to-all-start = ((f32[2,100,32,128]{3,0,1,2:T(2,128)}), f32[2,100,32,128]{3,0,1,2:T(2,128)S(1)}, u32[]{:S(2)}, u32[]{:S(2)}) async-start(f32[2,100,32,128]{3,0,1,2:T(2,128)} %copy.74), calls=%async_computation | async-start | bytes 6553600 | tf_op jit(solution)/shard_map/all_to_all | solution.py:101
  199.6 46.6 %all-to-all-start.1 = ((f32[32,100,2,128]{3,2,1,0:T(2,128)}), f32[32,100,2,128]{3,2,1,0:T(2,128)}, u32[]{:S(2)}, u32[]{:S(2)}) async-start(f32[32,100,2,128]{3,2,1,0:T(2,128)} %copy.78), calls=%async_computation.1 | async-start | bytes 6553600 | tf_op jit(solution)/shard_map/all_to_all | solution.py:72
  220.1 23.6 %copy-start.4 = (f32[25,8,32,128]{3,2,1,0:T(8,128)S(1)}, f32[25,8,32,128]{3,2,1,0:T(8,128)}, u32[]{:S(2)}) copy-start(f32[25,8,32,128]{3,2,1,0:T(8,128)} %copy-done.3) | copy-start | bytes 9830404
  254.3 1.4 copy-start.7
  254.3 2.4 copy-start.8
  255.2 2.7 copy-start.6
  305.2 97.5 %collective-permute-start.2 = (f32[2,100,32,128]{3,2,1,0:T(8,128)S(1)}, f32[2,100,32,128]{3,2,1,0:T(8,128)S(1)}, u32[]{:S(2)}, u32[]{:S(2)}) collective-permute-start(f32[2,100,32,128]{3,2,1,0:T(8,128)S(1)} %fusion.20), channel_id=1, source_target_pairs={{0,16},{16,32},{32,48},{48,64},{64,80},{80,96},{96,112},{112,128},... | collective-permute-start | bytes 9830408 | tf_op jit(solution)/shard_map/ppermute | solution.py:16
  367.2 40.0 %collective-permute-start.3 = (f32[2,100,32,128]{3,2,1,0:T(8,128)S(1)}, f32[2,100,32,128]{3,2,1,0:T(8,128)S(1)}, u32[]{:S(2)}, u32[]{:S(2)}) collective-permute-start(f32[2,100,32,128]{3,2,1,0:T(8,128)S(1)} %fusion.20), channel_id=1, source_target_pairs={{16,0},{32,16},{48,32},{64,48},{80,64},{96,80},{112,96},{128,112},... | collective-permute-start | bytes 9830408 | tf_op jit(solution)/shard_map/ppermute | solution.py:19
  407.2 8.0 %copy-start.1 = (f32[2,100,32,128]{3,2,1,0:T(8,128)S(1)}, f32[2,100,32,128]{3,2,1,0:T(8,128)}, u32[]{:S(2)}) copy-start(f32[2,100,32,128]{3,2,1,0:T(8,128)} %param.5) | copy-start | bytes 9830404
where the time goes:
time: 422 us; the launch traced here: 416 us
  local copies, waits for them, and re-layouts  131 us (31%)
  waiting for transfers between devices  126 us (30%)
  starting transfers between devices  86.6 us (21%)
  matrix products  41.1 us (10%)
  other arithmetic  30.3 us (7%)
    ppermute x2, waiting for transfers between devices, extended(): lax.ppermute(lax.slice_in_dim(block, block.shape[dim] - width, None, axis...  66.9 us
    ppermute x2, starting transfers between devices, extended(): lax.ppermute(lax.slice_in_dim(block, block.shape[dim] - width, None, axis...  66.4 us
    gather x4, local copies, waits for them, and re-layouts, reorder_cells(): reordered = jnp.take(flattened, positions, axis=0)  54.4 us
    all_to_all x1, waiting for transfers between devices, on_device(): lax.all_to_all(picked, 'member', split_axis=2, concat_axis=0, tiled=True)  54.1 us
    dot_general x2, matrix products, band_rows(): jnp.einsum('rp,mvpk->mvrk', lat_band, padded, precision=lax.Precision.HIG...  19 us
    scatter x1, local copies, waits for them, and re-layouts, on_device(): jnp.zeros((mesh_locations,), jnp.int32).at[order]  15.7 us
    unnamed x24, local copies, waits for them, and re-layouts  14.1 us
    all_to_all x1, starting transfers between devices, on_device(): lax.all_to_all(picked, 'member', split_axis=2, concat_axis=0, tiled=True)  11.4 us
  transfers between devices with their start and end apart: 6, of which 5 were waited for; matrix products, arithmetic and copies ran while one was open for 11% of the time, Pallas kernels for 0%

commit v1 on v0

--- a/solution.py
+++ b/solution.py
@@ -1,3 +1,4 @@
+import functools
 import jax
 import jax.numpy as jnp
 from jax import lax
@@ -6,6 +7,18 @@
 LON = 128
 HALF = 32
 PATCH = 128
+
+
+def review_the_run(array_here, mesh_ax, array_axis, dim_no):
+    return jnp.concatenate(
+        lax.all_to_all(
+            jnp.stack(jnp.split(array_here, lax.axis_size(mesh_ax), axis=array_axis)), mesh_ax, 0, 0
+        ),
+        axis=dim_no,
+    )
+
+
+return_all_tracks = functools.partial(review_the_run, mesh_ax="member", array_axis=0, dim_no=2)
 
 
 def extended(block, sides, width):
@@ -69,7 +82,7 @@
         "vkmn,nvkp->mvkp", pair_weights, gathered, precision=lax.Precision.HIGHEST
     )
     apart = apart / members
-    return lax.all_to_all(apart, "member", split_axis=0, concat_axis=2, tiled=True)
+    return return_all_tracks(apart)
 
 
 def reorder_cells(values, positions):

time: 422 us -> 432 us (1.024)
  the two profiles are of different devices: /device:TPU:1 before, /device:TPU:107 now
where the time goes in v1:
time: 432 us; the launch traced here: 426 us
  waiting for transfers between devices  181 us (42%)
  local copies, waits for them, and re-layouts  144 us (33%)
  matrix products  41.4 us (10%)
  other arithmetic  30.3 us (7%)
  starting transfers between devices  29.1 us (7%)
    all_to_all x1, waiting for transfers between devices, on_device(): lax.all_to_all(picked, 'member', split_axis=2, concat_axis=0, tiled=True)  75.6 us
    gather x4, local copies, waits for them, and re-layouts, reorder_cells(): reordered = jnp.take(flattened, positions, axis=0)  54.7 us
    ppermute x2, waiting for transfers between devices, extended(): lax.ppermute(lax.slice_in_dim(block, block.shape[dim] - width, None, axis...  50.9 us
    all_to_all x1, waiting for transfers between devices, review_the_run(): lax.all_to_all(jnp.stack(jnp.split(array_here, lax.axis_size(mesh_ax), ax...  49.7 us
    unnamed x39, local copies, waits for them, and re-layouts  26 us
    dot_general x2, matrix products, band_rows(): jnp.einsum('rp,mvpk->mvrk', lat_band, padded, precision=lax.Precision.HIG...  19 us
    scatter x1, local copies, waits for them, and re-layouts, on_device(): jnp.zeros((mesh_locations,), jnp.int32).at[order]  16.1 us
    all_to_all x1, starting transfers between devices, on_device(): lax.all_to_all(picked, 'member', split_axis=2, concat_axis=0, tiled=True)  9.38 us
  transfers between devices with their start and end apart: 6, of which 5 were waited for; matrix products, arithmetic and copies ran while one was open for 11% of the time, Pallas kernels for 0%

profile of v1, /device:TPU:107, one launch (start us, length us, event | category | flops | bytes accessed | tf_op | source)
XLA Modules:
  0.0 425.6 jit_solution(4941373419926805850)
XLA Ops:
  1.9 5.9 %fusion.14 = f32[2,100,32,128]{3,1,2,0:T(8,128)S(1)} fusion(f32[2,100,32,128]{3,2,1,0:T(8,128)S(1)} %copy-done, f32[]{:T(128)} %exponential_reduce_fusion), kind=kOutput, calls=%fused_computation.28 | convolution fusion | flops 1258504192 | bytes 6553604 | tf_op jit(solution)/shard_map/mvrl,lk->mvrk/dot_general | solution.py:63
  9.6 3.7 collective-permute-start
  15.3 16.1 %scatter_custom_fusion = s32[4096]{0:T(1024)S(1)} fusion(s32[4096]{0:T(1024)S(1)} %bitcast.165, s32[4096]{0:T(1024)S(1)} %iota.49, s32[]{:T(128)} %constant.26.clone.1), kind=kCustom, calls=%fused_computation.84 | custom fusion | bytes 16388 | tf_op jit(solution)/shard_map/scatter | solution.py:102
  31.4 17.5 %collective-permute-done = f32[2,100,32,128]{3,2,1,0:T(8,128)} collective-permute-done((f32[2,100,32,128]{3,2,1,0:T(8,128)S(1)}, f32[2,100,32,128]{3,2,1,0:T(8,128)}, u32[]{:S(2)}, u32[]{:S(2)}) %collective-permute-start) | collective-permute-done | bytes 3276832 | tf_op jit(solution)/shard_map/ppermute | solution.py:29
  48.9 5.5 %copy.64 = f32[2,100,32,128]{3,1,2,0:T(8,128)} copy(f32[2,100,32,128]{3,2,1,0:T(8,128)} %collective-permute-done) | data formatting | bytes 6553600 | tf_op jit(solution)/shard_map/ppermute | solution.py:29
  54.4 5.5 %copy.65 = f32[2,100,32,128]{3,1,2,0:T(8,128)} copy(f32[2,100,32,128]{3,2,1,0:T(8,128)} %collective-permute-done.1) | data formatting | bytes 6553600 | tf_op jit(solution)/shard_map/ppermute | solution.py:32
  60.0 8.5 %pad_maximum_fusion = f32[2,100,96,128]{3,1,2,0:T(8,128)} fusion(f32[2,100,32,128]{3,1,2,0:T(8,128)} %copy.65, f32[2,100,32,128]{3,1,2,0:T(8,128)} %copy-done.2, f32[2,100,32,128]{3,1,2,0:T(8,128)} %copy.64), kind=kLoop, calls=%fused_computation.4 | loop fusion | flops 4915200 | bytes 19660800 | tf_op jit(solution)/shard_map/concatenate | solution.py:33
  68.5 10.9 %fusion.6 = f32[2,100,128,32]{2,3,1,0:T(8,128)S(1)} fusion(f32[2,100,96,128]{3,1,2,0:T(8,128)} %pad_maximum_fusion, f32[]{:T(128)} %exponential_reduce_fusion, s32[96]{0:T(128)S(1)} %iota_add_fusion), kind=kOutput, calls=%fused_computation.11 | convolution fusion | flops 943758336 | bytes 13107588 | tf_op jit(solution)/shard_map/rp,mvpk->mvrk/dot_general | solution.py:59
  82.2 3.3 copy.67
  85.6 18.4 %gather_fusion.1 = f32[4096,200]{1,0:T(8,128)} fusion(f32[4096,200]{1,0:T(8,128)} %bitcast.147, s32[4096]{0:T(1024)S(1)} %get-tuple-element.8), kind=kCustom, calls=%fused_computation.clone | custom fusion | bytes 6569984 | tf_op jit(solution)/shard_map/jit(_take)/gather | solution.py:91
  104.0 3.7 copy.68
  110.2 4.2 copy.71
  114.5 9.4 %all-to-all-start = ((f32[2,100,32,128]{3,0,1,2:T(2,128)}), f32[2,100,32,128]{3,0,1,2:T(2,128)S(1)}, u32[]{:S(2)}, u32[]{:S(2)}) async-start(f32[2,100,32,128]{3,0,1,2:T(2,128)} %copy.71), calls=%async_computation | async-start | bytes 6553600 | tf_op jit(solution)/shard_map/all_to_all | solution.py:114
  123.9 75.6 %all-to-all-done = f32[2,100,32,128]{3,0,1,2:T(2,128)S(1)} async-done(((f32[2,100,32,128]{3,0,1,2:T(2,128)}), f32[2,100,32,128]{3,0,1,2:T(2,128)S(1)}, u32[]{:S(2)}, u32[]{:S(2)}) %all-to-all-start) | async-done | bytes 3276832 | tf_op jit(solution)/shard_map/all_to_all | solution.py:114
  204.3 6.2 %fusion.62 = (f32[100,2,32]{2,1,0:T(2,128)S(1)}, f32[100,2,32,32]{2,3,1,0:T(8,128)S(1)}) fusion(f32[32,100,2,128]{3,0,2,1:T(8,128)S(1)} %bitcast.150, f32[100,2,32]{2,1,0:T(2,128)S(1)} %multiply_reduce_fusion, pred[32,32]{0,1:T(8,128)(4,1)S(1)} %iota_compare_fusion), kind=kOutput, calls=%fused_computation.105 | convolution fusion | flops 316000000 | bytes 4148224 | tf_op jit(solution)/shard_map/mvkp,nvkp->vkmn/dot_general | solution.py:69
  210.6 6.9 %fusion.13 = f32[32,100,2,128]{3,0,2,1:T(8,128)S(1)} fusion(f32[32,100,2,128]{3,0,2,1:T(8,128)S(1)} %bitcast.151, f32[100,2,32,32]{2,3,1,0:T(8,128)S(1)} %get-tuple-element.7, f32[32,100,2]{0,2,1:T(2,128)S(1)} %bitcast.162), kind=kOutput, calls=%fused_computation.23 | convolution fusion | flops 317030400 | bytes 7398400 | tf_op jit(solution)/shard_map/vkmn,nvkp->mvkp/dot_general | solution.py:81
  230.1 8.0 %all-to-all-start.1 = ((f32[16,2,100,2,128]{4,1,3,2,0:T(2,128)}), f32[16,2,100,2,128]{4,1,3,2,0:T(2,128)}, u32[]{:S(2)}, u32[]{:S(2)}) async-start(f32[16,2,100,2,128]{4,1,3,2,0:T(2,128)} %fusion.20), calls=%async_computation.1 | async-start | bytes 6553600 | tf_op jit(solution)/shard_map/all_to_all | solution.py:14
  240.0 14.2 %gather_fusion = f32[4096,100]{1,0:T(8,128)} fusion(f32[4096,100]{1,0:T(8,128)S(1)} %bitcast.148, s32[4096]{0:T(1024)S(1)} %broadcast_clamp_fusion), kind=kCustom, calls=%fused_computation.2 | custom fusion | bytes 3293184 | tf_op jit(solution)/shard_map/jit(_take)/gather | solution.py:91
  254.2 4.8 %broadcast_select_fusion = f32[4096,100]{1,0:T(8,128)} fusion(f32[4096,100]{1,0:T(8,128)} %gather_fusion, pred[4096]{0:T(1024)(128)(4,1)S(1)} %compare_and_fusion.1), kind=kLoop, calls=%fused_computation.30 | loop fusion | flops 409600 | bytes 3280896 | tf_op jit(solution)/shard_map/jit(_take)/select_n | solution.py:91
  264.6 49.7 %all-to-all-done.1 = f32[16,2,100,2,128]{4,1,3,2,0:T(2,128)} async-done(((f32[16,2,100,2,128]{4,1,3,2,0:T(2,128)}), f32[16,2,100,2,128]{4,1,3,2,0:T(2,128)}, u32[]{:S(2)}, u32[]{:S(2)}) %all-to-all-start.1) | async-done | bytes 3276832 | tf_op jit(solution)/shard_map/all_to_all | solution.py:14
  314.3 3.6 copy.75
  318.0 4.3 %reshape.80 = f32[200,4096]{1,0:T(8,128)} reshape(f32[2,100,16,2,128]{4,3,2,1,0:T(2,128)S(1)} %copy.75) | data formatting | bytes 6553600 | tf_op jit(solution)/shard_map/reshape | solution.py:13
  325.9 8.6 %fusion.12 = f32[4096,200]{0,1:T(8,128)} fusion(f32[200,4096]{1,0:T(8,128)S(1)} %copy-done.8, f32[25,8,32,128]{3,2,1,0:T(8,128)S(1)} %bitcast.158, f32[25,8,32,128]{3,2,1,0:T(8,128)S(1)} %bitcast.159, f32[4096,200]{0,1:T(8,128)S(1)} %copy-done.6, pred[4096]{0:T(1024)(128)(4,1)S(1)} %compare_and_fusion.1), kind=kLoop, calls=%fused_computation.19 | loop fusion | flops 4096000 | bytes 16388096 | tf_op jit(solution)/shard_map/transpose | solution.py:90
  334.5 5.2 %copy.76 = f32[4096,200]{1,0:T(8,128)} copy(f32[4096,200]{0,1:T(8,128)} %fusion.12) | data formatting | bytes 6553600 | tf_op jit(solution)/shard_map/transpose | solution.py:90
  339.7 18.4 %gather_fusion.2 = f32[4096,200]{1,0:T(8,128)} fusion(f32[4096,200]{1,0:T(8,128)} %copy.76, s32[4096]{0:T(1024)S(1)} %get-tuple-element.9), kind=kCustom, calls=%fused_computation.1.clone | custom fusion | bytes 6569984 | tf_op jit(solution)/shard_map/jit(_take)/gather | solution.py:91
  358.1 3.9 select_bitcast_fusion
  362.0 5.3 %copy.77 = f32[200,4096]{1,0:T(8,128)} copy(f32[200,4096]{0,1:T(8,128)} %select_bitcast_fusion) | data formatting | bytes 6553600 | tf_op jit(solution)/shard_map/transpose | solution.py:92
  369.8 3.5 fusion.36
  373.3 3.9 collective-permute-start.2
  379.5 33.4 %collective-permute-done.2 = f32[2,100,32,128]{3,2,1,0:T(8,128)S(1)} collective-permute-done((f32[2,100,32,128]{3,2,1,0:T(8,128)S(1)}, f32[2,100,32,128]{3,2,1,0:T(8,128)S(1)}, u32[]{:S(2)}, u32[]{:S(2)}) %collective-permute-start.2) | collective-permute-done | bytes 3276832 | tf_op jit(solution)/shard_map/ppermute | solution.py:29
  412.9 4.4 %collective-permute-done.3 = f32[2,100,32,128]{3,2,1,0:T(8,128)S(1)} collective-permute-done((f32[2,100,32,128]{3,2,1,0:T(8,128)S(1)}, f32[2,100,32,128]{3,2,1,0:T(8,128)S(1)}, u32[]{:S(2)}, u32[]{:S(2)}) %collective-permute-start.3) | collective-permute-done | bytes 3276832 | tf_op jit(solution)/shard_map/ppermute | solution.py:32
  417.3 8.1 %fusion.17 = f32[2,100,32,128]{3,2,1,0:T(8,128)} fusion(f32[2,100,32,128]{3,2,1,0:T(8,128)S(1)} %collective-permute-done.3, f32[2,100,32,128]{3,2,1,0:T(8,128)S(1)} %fusion.36, f32[2,100,32,128]{3,2,1,0:T(8,128)S(1)} %collective-permute-done.2, f32[]{:T(128)} %exponential_reduce_fusion, s32[96]{0:T(128)S(1)} %iota_add_fusion), kind=kOutput, calls=%fused_computation.29 | convolution fusion | flops 948673536 | bytes 13107588 | tf_op jit(solution)/shard_map/rp,mvpk->mvrk/dot_general | solution.py:59
  (62 shorter events, 44.3 us)
Async XLA Ops:
  0.0 1.9 copy-start
  7.8 1.8 copy-start.2
  7.8 7.4 %copy-start.9 = (s32[1,4096]{1,0:T(1,128)S(1)}, s32[1,4096]{1,0:T(1,128)}, u32[]{:S(2)}) copy-start(s32[1,4096]{1,0:T(1,128)} %param.7) | copy-start | bytes 49156
  9.6 39.3 %collective-permute-start = (f32[2,100,32,128]{3,2,1,0:T(8,128)S(1)}, f32[2,100,32,128]{3,2,1,0:T(8,128)}, u32[]{:S(2)}, u32[]{:S(2)}) collective-permute-start(f32[2,100,32,128]{3,2,1,0:T(8,128)S(1)} %copy.62), channel_id=1, source_target_pairs={{0,16},{16,32},{32,48},{48,64},{64,80},{80,96},{96,112},{112,128},... | collective-permute-start | bytes 9830408 | tf_op jit(solution)/shard_map/ppermute | solution.py:29
  13.3 41.1 %collective-permute-start.1 = (f32[2,100,32,128]{3,2,1,0:T(8,128)S(1)}, f32[2,100,32,128]{3,2,1,0:T(8,128)}, u32[]{:S(2)}, u32[]{:S(2)}) collective-permute-start(f32[2,100,32,128]{3,2,1,0:T(8,128)S(1)} %copy.62), channel_id=1, source_target_pairs={{16,0},{32,16},{48,32},{64,48},{80,64},{96,80},{112,96},{128,112},... | collective-permute-start | bytes 9830408 | tf_op jit(solution)/shard_map/ppermute | solution.py:32
  107.7 1.7 copy-start.5
  110.2 4.2 copy-start.3
  114.5 85.0 %all-to-all-start = ((f32[2,100,32,128]{3,0,1,2:T(2,128)}), f32[2,100,32,128]{3,0,1,2:T(2,128)S(1)}, u32[]{:S(2)}, u32[]{:S(2)}) async-start(f32[2,100,32,128]{3,0,1,2:T(2,128)} %copy.71), calls=%async_computation | async-start | bytes 6553600 | tf_op jit(solution)/shard_map/all_to_all | solution.py:114
  230.1 84.2 %all-to-all-start.1 = ((f32[16,2,100,2,128]{4,1,3,2,0:T(2,128)}), f32[16,2,100,2,128]{4,1,3,2,0:T(2,128)}, u32[]{:S(2)}, u32[]{:S(2)}) async-start(f32[16,2,100,2,128]{4,1,3,2,0:T(2,128)} %fusion.20), calls=%async_computation.1 | async-start | bytes 6553600 | tf_op jit(solution)/shard_map/all_to_all | solution.py:14
  254.2 8.0 %copy-start.4 = (f32[25,8,32,128]{3,2,1,0:T(8,128)S(1)}, f32[25,8,32,128]{3,2,1,0:T(8,128)}, u32[]{:S(2)}) copy-start(f32[25,8,32,128]{3,2,1,0:T(8,128)} %copy-done.3) | copy-start | bytes 9830404
  322.3 1.4 copy-start.7
  322.3 2.4 copy-start.8
  323.2 2.7 copy-start.6
  373.3 39.5 %collective-permute-start.2 = (f32[2,100,32,128]{3,2,1,0:T(8,128)S(1)}, f32[2,100,32,128]{3,2,1,0:T(8,128)S(1)}, u32[]{:S(2)}, u32[]{:S(2)}) collective-permute-start(f32[2,100,32,128]{3,2,1,0:T(8,128)S(1)} %fusion.36), channel_id=1, source_target_pairs={{0,16},{16,32},{32,48},{48,64},{64,80},{80,96},{96,112},{112,128},... | collective-permute-start | bytes 9830408 | tf_op jit(solution)/shard_map/ppermute | solution.py:29
  377.3 40.0 %collective-permute-start.3 = (f32[2,100,32,128]{3,2,1,0:T(8,128)S(1)}, f32[2,100,32,128]{3,2,1,0:T(8,128)S(1)}, u32[]{:S(2)}, u32[]{:S(2)}) collective-permute-start(f32[2,100,32,128]{3,2,1,0:T(8,128)S(1)} %fusion.36), channel_id=1, source_target_pairs={{16,0},{32,16},{48,32},{64,48},{80,64},{96,80},{112,96},{128,112},... | collective-permute-start | bytes 9830408 | tf_op jit(solution)/shard_map/ppermute | solution.py:32
  417.3 8.1 %copy-start.1 = (f32[2,100,32,128]{3,2,1,0:T(8,128)S(1)}, f32[2,100,32,128]{3,2,1,0:T(8,128)}, u32[]{:S(2)}) copy-start(f32[2,100,32,128]{3,2,1,0:T(8,128)} %param.5) | copy-start | bytes 9830404
